TPU v7x, 32 devices: a whole 2x2x4 slice. The times are simulated.
32 devices in a mesh: groups: 2 (over y), tok: 16 (over z, x, core).
Axes of the slice: x: 2, y: 2, z: 4, core: 2. Of those that a mesh axis runs over, the one named last changes fastest.
Arguments:
- query_rows: bfloat16 [8192, 768], P(('groups', 'tok')), parts along dimension 0, may hold values from -6 to 6
- key_rows: bfloat16 [8192, 768], P(('groups', 'tok')), parts along dimension 0, may hold values from -6 to 6
- value_rows: bfloat16 [8192, 768], P(('groups', 'tok')), parts along dimension 0, may hold values from -6 to 6
- out_rows: bfloat16 [8192, 768], P(('groups', 'tok')), parts along dimension 0, may hold values from -6 to 6
- grad_out: bfloat16 [8192, 768], P(('groups', 'tok')), parts along dimension 0, may hold values from -6 to 6
- normalizer: float32 [16, 8192], P(None, ('groups', 'tok')), parts along dimension 1, may hold values from 3 to 5
- keep_tasks: int32 [32, 5], P('groups'), parts along dimension 0, may hold values from 0 to 1, as said below
Outputs:
- grad_query: bfloat16 [8192, 768], P(('groups', 'tok')), parts along dimension 0
- grad_key: bfloat16 [8192, 768], P(('groups', 'tok')), parts along dimension 0
- grad_value: bfloat16 [8192, 768], P(('groups', 'tok')), parts along dimension 0
There are 2 independent parts, one for each index of `groups`. A program takes and returns all parts, laid end to end along the dimension named above; each array names one. Nothing has to cross between parts.
Inputs may be any that keep to these rules, and one draw needn't show every extreme that they name: keep_tasks[a, 2] = 1 for every block a; entries naming a key block outside 0 to 15 are ignored.
All inputs are finite; a program needn't handle non-finite values.
Results may differ from a plain program's by a relative error of at most 0.0053.
Values may be sent and summed in bfloat16 or wider, within the bound.
A program may use at most 128 MiB of HBM per device.

v0:
```python
import jax
import jax.numpy as jnp
from jax import lax
from jax.sharding import PartitionSpec as P

HEADS = 16
RADIUS = 2
WIN = 5


def shifted(value, axis, steps):
    count = lax.axis_size(axis)
    first, last = (max(0, -steps), min(count, count - steps))
    return lax.ppermute(value, axis, [(source, source + steps) for source in range(first, last)])


def split_heads(rows_in):
    return rows_in.reshape(rows_in.shape[0], HEADS, rows_in.shape[1] // HEADS)


def block_delta(dout_rows, out_rows):
    product = split_heads(dout_rows).astype(jnp.float32) * split_heads(out_rows).astype(jnp.float32)
    return jnp.transpose(jnp.sum(product, axis=2))


def scores_grads(query_rows, dout_rows, lse_rows, delta_rows, key_block, value_block, scale):
    q_heads = split_heads(query_rows)
    dout_heads = split_heads(dout_rows)
    k_heads = split_heads(key_block)
    v_heads = split_heads(value_block)
    scores = (
        jnp.einsum("qhe,khe->hqk", q_heads, k_heads, preferred_element_type=jnp.float32) * scale
    )
    probs = jnp.exp(scores - lse_rows[:, :, None])
    prob_grad = jnp.einsum("qhe,khe->hqk", dout_heads, v_heads, preferred_element_type=jnp.float32)
    score_grad = (probs * (prob_grad - delta_rows[:, :, None])).astype(jnp.bfloat16)
    probs_low = probs.astype(jnp.bfloat16)
    return (q_heads, dout_heads, k_heads, probs_low, score_grad)


def grad_of_query(parts, scale):
    q_heads, dout_heads, k_heads, probs_low, score_grad = parts
    term = (
        jnp.einsum("hqk,khe->qhe", score_grad, k_heads, preferred_element_type=jnp.float32) * scale
    )
    return term.reshape(term.shape[0], term.shape[1] * term.shape[2])


def grads_of_keys(parts, scale):
    q_heads, dout_heads, k_heads, probs_low, score_grad = parts
    term_k = (
        jnp.einsum("hqk,qhe->khe", score_grad, q_heads, preferred_element_type=jnp.float32) * scale
    )
    term_v = jnp.einsum("hqk,qhe->khe", probs_low, dout_heads, preferred_element_type=jnp.float32)
    stacked = jnp.stack([term_k, term_v])
    return stacked.reshape(2, term_k.shape[0], term_k.shape[1] * term_k.shape[2])


def task_flag(keep_tasks, block, offset_index, count):
    target = block - RADIUS + offset_index
    inside = (block >= 0) & (block < count) & (target >= 0) & (target < count)
    return jnp.where(inside, keep_tasks[jnp.clip(block, 0, count - 1), offset_index], 0)


def per_device(query_rows, key_rows, value_rows, out_rows, grad_out, normalizer, keep_tasks):
    rows, width = query_rows.shape
    scale = (width // HEADS) ** (-0.5)
    count = lax.axis_size("tok")
    place = lax.axis_index("tok")
    delta = block_delta(grad_out, out_rows)
    pairs = jnp.stack([key_rows, value_rows])
    zero_rows = jnp.zeros((rows, width), jnp.float32)
    zero_pair = jnp.zeros((2, rows, width), jnp.float32)
    grad_query = zero_rows
    grad_pair = zero_pair

    def whole(keys_in):
        parts = scores_grads(query_rows, grad_out, normalizer, delta, keys_in[0], keys_in[1], scale)
        return (grad_of_query(parts, scale), grads_of_keys(parts, scale))

    def nothing(unused):
        return (zero_rows, zero_pair)

    for j in range(WIN):
        offset = j - RADIUS
        if offset == 0:
            keys_here = pairs
        else:
            keys_here = shifted(pairs, "tok", -offset)
        own_flag = task_flag(keep_tasks, place, j, count)
        term_q, term_k = lax.cond(own_flag > 0, whole, nothing, keys_here)
        grad_query = grad_query + term_q
        if offset == 0:
            grad_pair = grad_pair + term_k
        else:
            grad_pair = grad_pair + shifted(term_k, "tok", offset)
    return (
        grad_query.astype(jnp.bfloat16),
        grad_pair[0].astype(jnp.bfloat16),
        grad_pair[1].astype(jnp.bfloat16),
    )


def solution(mesh):
    return jax.shard_map(
        per_device,
        mesh=mesh,
        in_specs=(
            P(("groups", "tok"), None),
            P(("groups", "tok"), None),
            P(("groups", "tok"), None),
            P(("groups", "tok"), None),
            P(("groups", "tok"), None),
            P(None, ("groups", "tok")),
            P("groups", None),
        ),
        out_specs=(
            P(("groups", "tok"), None),
            P(("groups", "tok"), None),
            P(("groups", "tok"), None),
        ),
        check_vma=False,
    )
```

profile of v0, /device:TPU:9, one launch (start us, length us, event | category | flops | bytes accessed | tf_op | source)
XLA Modules:
  0.0 202.5 jit_solution(5160384420963412973)
XLA Ops:
  0.7 1.2 copy.34
  1.9 1.2 copy.35
  3.1 1.0 pad_maximum_fusion.5
  4.0 3.1 %collective-permute-start.3 = (bf16[2,256,768]{1,2,0:T(8,128)(2,1)}, bf16[2,256,768]{1,2,0:T(8,128)(2,1)S(1)}, u32[]{:S(2)}, u32[]{:S(2)}) collective-permute-start(bf16[2,256,768]{1,2,0:T(8,128)(2,1)} %pad_maximum_fusion.5), channel_id=1, source_target_pairs={{2,0},{3,1},{4,2},{5,3},{6,4},{7,5},{8,6},{9,7},{10,8},{11,9},{12,... | collective-permute-start | bytes 2359304 | tf_op jit(solution)/shard_map/ppermute | solution.py:14
  7.2 2.9 %collective-permute-start.2 = (bf16[2,256,768]{1,2,0:T(8,128)(2,1)}, bf16[2,256,768]{1,2,0:T(8,128)(2,1)}, u32[]{:S(2)}, u32[]{:S(2)}) collective-permute-start(bf16[2,256,768]{1,2,0:T(8,128)(2,1)} %pad_maximum_fusion.5), channel_id=1, source_target_pairs={{1,0},{2,1},{3,2},{4,3},{5,4},{6,5},{7,6},{8,7},{9,8},{10,9},{11,1... | collective-permute-start | bytes 2359304 | tf_op jit(solution)/shard_map/ppermute | solution.py:14
  10.0 2.7 %collective-permute-start.1 = (bf16[2,256,768]{1,2,0:T(8,128)(2,1)}, bf16[2,256,768]{1,2,0:T(8,128)(2,1)}, u32[]{:S(2)}, u32[]{:S(2)}) collective-permute-start(bf16[2,256,768]{1,2,0:T(8,128)(2,1)} %pad_maximum_fusion.5), channel_id=1, source_target_pairs={{0,1},{1,2},{2,3},{3,4},{4,5},{5,6},{6,7},{7,8},{8,9},{9,10},{10,1... | collective-permute-start | bytes 2359304 | tf_op jit(solution)/shard_map/ppermute | solution.py:14
  12.8 3.5 %collective-permute-start = (bf16[2,256,768]{1,2,0:T(8,128)(2,1)}, bf16[2,256,768]{1,2,0:T(8,128)(2,1)}, u32[]{:S(2)}, u32[]{:S(2)}) collective-permute-start(bf16[2,256,768]{1,2,0:T(8,128)(2,1)} %pad_maximum_fusion.5), channel_id=1, source_target_pairs={{0,2},{1,3},{2,4},{3,5},{4,6},{5,7},{6,8},{7,9},{8,10},{9,11},{10,... | collective-permute-start | bytes 2359304 | tf_op jit(solution)/shard_map/ppermute | solution.py:14
  16.3 0.6 constant_dynamic-slice_fusion.3
  19.5 0.2 copy.37
  19.7 0.2 copy.36
  20.0 29.9 %collective-permute-done.3 = bf16[2,256,768]{1,2,0:T(8,128)(2,1)S(1)} collective-permute-done((bf16[2,256,768]{1,2,0:T(8,128)(2,1)}, bf16[2,256,768]{1,2,0:T(8,128)(2,1)S(1)}, u32[]{:S(2)}, u32[]{:S(2)}) %collective-permute-start.3) | collective-permute-done | bytes 786464 | tf_op jit(solution)/shard_map/ppermute | solution.py:14
  50.0 8.7 %conditional.9 = (f32[2,256,768]{1,2,0:T(8,128)S(1)}, f32[256,768]{1,0:T(8,128)}) conditional(s32[]{:T(128)} %convert_element_type.70, () %tuple.56, (bf16[256,768]{1,0:T(8,128)(2,1)S(1)}, bf16[2,256,768]{1,2,0:T(8,128)(2,1)S(1)}, f32[16,256]{1,0:T(8,128)S(1)}, bf16[256,768]{1,0:T(8,128)(2,1)S(1)}, f32[16,256]{1,0:T(8,128)S(1)}) %tuple.116), branch_computations={%region_9.10_spmd, %region_10.11_spmd} | conditional | flops 512491520 | bytes 31899664 | solution.py:91
  50.0 0.2 copy.53
  50.2 0.2 copy.52
  50.4 0.8 fusion.38
  51.1 1.9 fusion.25
  53.0 2.0 multiply_convert_fusion.4
  55.0 0.5 convolution_multiply_fusion.8
  55.5 0.7 convolution_multiply_fusion.9
  56.3 1.2 copy.71
  57.4 1.2 pad_maximum_fusion.4
  58.7 1.7 copy.59
  60.3 9.8 %conditional.8 = (f32[2,256,768]{1,2,0:T(8,128)S(1)}, f32[256,768]{1,0:T(8,128)}) conditional(s32[]{:T(128)} %convert_element_type.69, () %tuple.54, (bf16[256,768]{1,0:T(8,128)(2,1)S(1)}, bf16[2,256,768]{1,2,0:T(8,128)(2,1)}, f32[16,256]{1,0:T(8,128)S(1)}, bf16[256,768]{1,0:T(8,128)(2,1)S(1)}, f32[16,256]{1,0:T(8,128)S(1)}) %tuple.117), branch_computations={%region_7.8_spmd, %region_8.9_spmd} | conditional | flops 512491520 | bytes 31899664 | solution.py:91
  60.5 0.2 copy.49
  60.7 1.2 fusion.32
  61.8 0.8 fusion.37
  62.6 1.9 fusion.19
  64.5 2.0 multiply_convert_fusion.3
  66.5 0.5 convolution_multiply_fusion.6
  67.0 0.7 convolution_multiply_fusion.7
  67.7 1.2 copy.69
  68.9 1.2 pad_maximum_fusion.3
  70.1 1.6 copy.58
  71.7 9.8 %conditional.6 = (f32[2,256,768]{1,2,0:T(8,128)S(1)}, f32[256,768]{1,0:T(8,128)}) conditional(s32[]{:T(128)} %convert_element_type.67, () %tuple.50, (bf16[256,768]{1,0:T(8,128)(2,1)S(1)}, bf16[2,256,768]{1,2,0:T(8,128)(2,1)}, f32[16,256]{1,0:T(8,128)S(1)}, bf16[256,768]{1,0:T(8,128)(2,1)S(1)}, f32[16,256]{1,0:T(8,128)S(1)}) %tuple.118), branch_computations={%region_3.4_spmd, %region_4.5_spmd} | conditional | flops 512491520 | bytes 31899664 | solution.py:91
  72.1 1.2 fusion.31
  73.3 0.8 fusion.36
  74.0 1.9 fusion.7
  75.9 2.0 multiply_convert_fusion.1
  77.9 0.5 convolution_multiply_fusion.2
  78.4 0.7 convolution_multiply_fusion.3
  79.2 1.2 copy.63
  80.3 1.2 pad_maximum_fusion.1
  81.6 1.6 copy.56
  83.2 1.3 conditional.5
  83.2 1.0 broadcast_in_dim.20.clone
  84.5 1.6 copy.55
  86.2 1.9 collective-permute-start.4
  88.1 12.0 %collective-permute-start.5 = (f32[2,256,768]{2,1,0:T(8,128)}, f32[2,256,768]{2,1,0:T(8,128)}, u32[]{:S(2)}, u32[]{:S(2)}) collective-permute-start(f32[2,256,768]{2,1,0:T(8,128)} %copy.56), channel_id=1, source_target_pairs={{1,0},{2,1},{3,2},{4,3},{5,4},{6,5},{7,6},{8,7},{9,8},{10,9},{11,1... | collective-permute-start | bytes 4718600 | tf_op jit(solution)/shard_map/ppermute | solution.py:14
  100.1 3.5 %collective-permute-start.6 = (f32[2,256,768]{2,1,0:T(8,128)}, f32[2,256,768]{2,1,0:T(8,128)}, u32[]{:S(2)}, u32[]{:S(2)}) collective-permute-start(f32[2,256,768]{2,1,0:T(8,128)} %copy.58), channel_id=1, source_target_pairs={{0,1},{1,2},{2,3},{3,4},{4,5},{5,6},{6,7},{7,8},{8,9},{9,10},{10,1... | collective-permute-start | bytes 4718600 | tf_op jit(solution)/shard_map/ppermute | solution.py:14
  103.6 2.0 collective-permute-start.7
  106.3 9.1 %conditional.7 = (f32[256,768]{1,0:T(8,128)}, f32[2,256,768]{2,1,0:T(8,128)S(1)}) conditional(s32[]{:T(128)} %convert_element_type.68, () %tuple.52, (bf16[256,768]{1,0:T(8,128)(2,1)S(1)}, bf16[256,768]{1,0:T(8,128)(2,1)}, f32[16,256]{1,0:T(8,128)S(1)}, bf16[256,768]{1,0:T(8,128)(2,1)S(1)}, bf16[256,768]{1,0:T(8,128)(2,1)S(1)}, ...), branch_computations={%region_5.6_spmd, %region_6.7_spmd} | conditional | flops 512491520 | bytes 35110956 | solution.py:91
  106.7 1.2 copy.45
  108.0 0.7 fusion.34
  108.8 1.6 fusion.13
  110.4 2.0 multiply_convert_fusion.2
  112.4 0.5 convolution_multiply_fusion.4
  112.9 0.7 convolution_multiply_fusion.5
  113.7 1.1 copy.65
  114.9 0.5 copy.67
  115.4 3.0 %add_convert_fusion.1 = bf16[256,768]{1,0:T(8,128)(2,1)} fusion(f32[256,768]{1,0:T(8,128)} %get-tuple-element.158, f32[256,768]{1,0:T(8,128)} %get-tuple-element.157, f32[256,768]{1,0:T(8,128)} %get-tuple-element.155, f32[256,768]{1,0:T(8,128)} %get-tuple-element.153, f32[256,768]{1,0:T(8,128)} %get-tuple-element.154), kind=kLoop, calls=%fused_computation.52 | loop fusion | flops 983040 | bytes 4325376 | tf_op jit(solution)/shard_map/convert_element_type | solution.py:98
  118.4 59.3 %collective-permute-done.4 = f32[2,256,768]{2,1,0:T(8,128)} collective-permute-done((f32[2,256,768]{2,1,0:T(8,128)}, f32[2,256,768]{2,1,0:T(8,128)}, u32[]{:S(2)}, u32[]{:S(2)}) %collective-permute-start.4) | collective-permute-done | bytes 1572896 | tf_op jit(solution)/shard_map/ppermute | solution.py:14
  177.7 20.6 %collective-permute-done.5 = f32[2,256,768]{2,1,0:T(8,128)} collective-permute-done((f32[2,256,768]{2,1,0:T(8,128)}, f32[2,256,768]{2,1,0:T(8,128)}, u32[]{:S(2)}, u32[]{:S(2)}) %collective-permute-start.5) | collective-permute-done | bytes 1572896 | tf_op jit(solution)/shard_map/ppermute | solution.py:14
  198.4 3.2 %add_convert_fusion = bf16[2,256,768]{2,1,0:T(8,128)(2,1)S(1)} fusion(f32[2,256,768]{2,1,0:T(8,128)} %collective-permute-done.7, f32[2,256,768]{2,1,0:T(8,128)} %collective-permute-done.6, f32[2,256,768]{2,1,0:T(8,128)S(1)} %get-tuple-element.156, f32[2,256,768]{2,1,0:T(8,128)} %collective-permute-done.4, f32[2,256,768]{2,1,0:T(8,128)} %collective-permute-done.5), kind=kLoop, calls=%fused_computation.50 | loop fusion | flops 1966080 | bytes 8650752 | tf_op jit(solution)/shard_map/convert.1
  201.6 0.9 slice_bitcast_fusion
  (32 shorter events, 1.5 us)
Async XLA Ops:
  0.6 15.6 %copy-start.7 = (s32[16,5]{0,1:T(8,128)S(1)}, s32[16,5]{0,1:T(8,128)}, u32[]{:S(2)}) copy-start(s32[16,5]{0,1:T(8,128)} %param.23) | copy-start | bytes 964
  0.6 18.8 %copy-start.6 = (bf16[256,768]{1,0:T(8,128)(2,1)S(1)}, bf16[256,768]{1,0:T(8,128)(2,1)}, u32[]{:S(2)}) copy-start(bf16[256,768]{1,0:T(8,128)(2,1)} %param.20) | copy-start | bytes 1179652
  0.7 19.0 %copy-start = (bf16[256,768]{1,0:T(8,128)(2,1)S(1)}, bf16[256,768]{1,0:T(8,128)(2,1)}, u32[]{:S(2)}) copy-start(bf16[256,768]{1,0:T(8,128)(2,1)} %param.21) | copy-start | bytes 1179652
  4.0 45.9 %copy-start.1 = (bf16[256,768]{1,0:T(8,128)(2,1)S(1)}, bf16[256,768]{1,0:T(8,128)(2,1)}, u32[]{:S(2)}) copy-start(bf16[256,768]{1,0:T(8,128)(2,1)} %param.17) | copy-start | bytes 1179652
  4.0 45.9 %copy-start.2 = (f32[16,256]{1,0:T(8,128)S(1)}, f32[16,256]{1,0:T(8,128)}, u32[]{:S(2)}) copy-start(f32[16,256]{1,0:T(8,128)} %param.22) | copy-start | bytes 49156
  4.0 45.9 %collective-permute-start.3 = (bf16[2,256,768]{1,2,0:T(8,128)(2,1)}, bf16[2,256,768]{1,2,0:T(8,128)(2,1)S(1)}, u32[]{:S(2)}, u32[]{:S(2)}) collective-permute-start(bf16[2,256,768]{1,2,0:T(8,128)(2,1)} %pad_maximum_fusion.5), channel_id=1, source_target_pairs={{2,0},{3,1},{4,2},{5,3},{6,4},{7,5},{8,6},{9,7},{10,8},{11,9},{12,... | collective-permute-start | bytes 2359304 | tf_op jit(solution)/shard_map/ppermute | solution.py:14
  7.2 53.2 %collective-permute-start.2 = (bf16[2,256,768]{1,2,0:T(8,128)(2,1)}, bf16[2,256,768]{1,2,0:T(8,128)(2,1)}, u32[]{:S(2)}, u32[]{:S(2)}) collective-permute-start(bf16[2,256,768]{1,2,0:T(8,128)(2,1)} %pad_maximum_fusion.5), channel_id=1, source_target_pairs={{1,0},{2,1},{3,2},{4,3},{5,4},{6,5},{7,6},{8,7},{9,8},{10,9},{11,1... | collective-permute-start | bytes 2359304 | tf_op jit(solution)/shard_map/ppermute | solution.py:14
  10.0 61.7 %collective-permute-start.1 = (bf16[2,256,768]{1,2,0:T(8,128)(2,1)}, bf16[2,256,768]{1,2,0:T(8,128)(2,1)}, u32[]{:S(2)}, u32[]{:S(2)}) collective-permute-start(bf16[2,256,768]{1,2,0:T(8,128)(2,1)} %pad_maximum_fusion.5), channel_id=1, source_target_pairs={{0,1},{1,2},{2,3},{3,4},{4,5},{5,6},{6,7},{7,8},{8,9},{9,10},{10,1... | collective-permute-start | bytes 2359304 | tf_op jit(solution)/shard_map/ppermute | solution.py:14
  12.8 70.5 %collective-permute-start = (bf16[2,256,768]{1,2,0:T(8,128)(2,1)}, bf16[2,256,768]{1,2,0:T(8,128)(2,1)}, u32[]{:S(2)}, u32[]{:S(2)}) collective-permute-start(bf16[2,256,768]{1,2,0:T(8,128)(2,1)} %pad_maximum_fusion.5), channel_id=1, source_target_pairs={{0,2},{1,3},{2,4},{3,5},{4,6},{5,7},{6,8},{7,9},{8,10},{9,11},{10,... | collective-permute-start | bytes 2359304 | tf_op jit(solution)/shard_map/ppermute | solution.py:14
  20.0 63.2 %copy-start.4 = (f32[256,16]{0,1:T(8,128)}, f32[256,16]{0,1:T(8,128)S(1)}, u32[]{:S(2)}) copy-start(f32[256,16]{0,1:T(8,128)S(1)} %reduce_sum.9) | copy-start | bytes 49156
  84.5 21.8 %copy-start.3 = (bf16[256,768]{1,0:T(8,128)(2,1)S(1)}, bf16[256,768]{1,0:T(8,128)(2,1)}, u32[]{:S(2)}) copy-start(bf16[256,768]{1,0:T(8,128)(2,1)} %param.19) | copy-start | bytes 1179652
  86.2 91.6 %collective-permute-start.4 = (f32[2,256,768]{2,1,0:T(8,128)}, f32[2,256,768]{2,1,0:T(8,128)}, u32[]{:S(2)}, u32[]{:S(2)}) collective-permute-start(f32[2,256,768]{2,1,0:T(8,128)} %copy.55), channel_id=1, source_target_pairs={{2,0},{3,1},{4,2},{5,3},{6,4},{7,5},{8,6},{9,7},{10,8},{11,9},{12,... | collective-permute-start | bytes 4718600 | tf_op jit(solution)/shard_map/ppermute | solution.py:14
  88.1 110.3 %collective-permute-start.5 = (f32[2,256,768]{2,1,0:T(8,128)}, f32[2,256,768]{2,1,0:T(8,128)}, u32[]{:S(2)}, u32[]{:S(2)}) collective-permute-start(f32[2,256,768]{2,1,0:T(8,128)} %copy.56), channel_id=1, source_target_pairs={{1,0},{2,1},{3,2},{4,3},{5,4},{6,5},{7,6},{8,7},{9,8},{10,9},{11,1... | collective-permute-start | bytes 4718600 | tf_op jit(solution)/shard_map/ppermute | solution.py:14
  100.1 98.3 %collective-permute-start.6 = (f32[2,256,768]{2,1,0:T(8,128)}, f32[2,256,768]{2,1,0:T(8,128)}, u32[]{:S(2)}, u32[]{:S(2)}) collective-permute-start(f32[2,256,768]{2,1,0:T(8,128)} %copy.58), channel_id=1, source_target_pairs={{0,1},{1,2},{2,3},{3,4},{4,5},{5,6},{6,7},{7,8},{8,9},{9,10},{10,1... | collective-permute-start | bytes 4718600 | tf_op jit(solution)/shard_map/ppermute | solution.py:14
  103.6 94.7 %collective-permute-start.7 = (f32[2,256,768]{2,1,0:T(8,128)}, f32[2,256,768]{2,1,0:T(8,128)}, u32[]{:S(2)}, u32[]{:S(2)}) collective-permute-start(f32[2,256,768]{2,1,0:T(8,128)} %copy.59), channel_id=1, source_target_pairs={{0,2},{1,3},{2,4},{3,5},{4,6},{5,7},{6,8},{7,9},{8,10},{9,11},{10,... | collective-permute-start | bytes 4718600 | tf_op jit(solution)/shard_map/ppermute | solution.py:14
  108.8 1.6 copy-start.5
where the time goes:
time: 204 us; the launch traced here: 203 us
  waiting for transfers between devices  110 us (54%)
  starting transfers between devices  31.6 us (15%)
  matrix products  23.2 us (11%)
  local copies, waits for them, and re-layouts  22.2 us (11%)
  other arithmetic  11.2 us (5%)
  between operations  4.06 us (2%)
    ppermute x8, waiting for transfers between devices, shifted(): lax.ppermute(value, axis, [(source, source + steps) for source in range(f...  110 us
    ppermute x8, starting transfers between devices, shifted(): lax.ppermute(value, axis, [(source, source + steps) for source in range(f...  31.6 us
    cond x9, local copies, waits for them, and re-layouts, per_device(): term_q, term_k = lax.cond(own_flag > 0, whole, nothing, keys_here)  11.7 us
    dot_general x4, matrix products, scores_grads(): jnp.einsum('qhe,khe->hqk', dout_heads, v_heads, preferred_element_type=jn...  7.99 us
    dot_general x4, matrix products, grads_of_keys(): jnp.einsum('hqk,qhe->khe', probs_low, dout_heads, preferred_element_type=...  7.31 us
  transfers between devices with their start and end apart: 8, of which 3 were waited for; matrix products, arithmetic and copies ran while one was open for 23% of the time, Pallas kernels for 0%

commit v1 on v0

v1 whole, which is shorter than its diff:
```python
import functools

import jax
import jax.numpy as jnp
from jax import lax
from jax.experimental import pallas as pl
from jax.experimental.pallas import tpu as pltpu
from jax.sharding import PartitionSpec as P

HEADS = 16
ROW = 4
PER = HEADS // ROW
LOG2E = 1.4426950408889634
MESH = pl.DeviceIdType.MESH
F32 = jnp.float32
BF16 = jnp.bfloat16


def dot_nn(a, b):
    return lax.dot_general(a, b, (((1,), (0,)), ((), ())), preferred_element_type=F32)


def dot_nt(a, b):
    return lax.dot_general(a, b, (((1,), (1,)), ((), ())), preferred_element_type=F32)


def kernel(
    count, q_ref, k_ref, v_ref, o_ref, g_ref, lse_ref, keep_ref,
    dq_out, dk_out, dv_out,
    kown, qown, sown, kbuf, qbuf, sbuf, dq, dkv, dqs, dqr, obuf, orecv,
    ks, kr, qs, qr, ss, sr, zs, zr, zss, zsr, ds, dr, os, orr,
):
    tok = lax.axis_index("tok")
    row, me = tok // ROW, tok % ROW
    rows = count // ROW
    has_low, has_high = row > 0, row < rows - 1
    width = q_ref.shape[1]
    dim = width // HEADS
    scale = dim ** -0.5

    barrier = pltpu.get_barrier_semaphore()

    def greet(target):
        pl.semaphore_signal(barrier, inc=1, device_id={"tok": target}, device_id_type=MESH)

    def mate(d):
        return row * ROW + (me + d) % ROW

    for d in range(1, ROW):
        greet(mate(d))

    @pl.when(has_low)
    def _():
        greet(tok - ROW)

    @pl.when(has_high)
    def _():
        greet(tok + ROW)

    def flipped(ref):
        return ref[...].T.reshape(HEADS, dim, ref.shape[0])

    qown[:, 0] = flipped(q_ref)
    g_t = flipped(g_ref)
    qown[:, 1] = g_t
    kown[:, 0] = flipped(k_ref)
    kown[:, 1] = flipped(v_ref)
    delta = jnp.sum(g_t.astype(F32) * flipped(o_ref).astype(F32), axis=1)
    lse2 = lse_ref[...] * LOG2E
    for j in range(ROW):
        sown[j, 0:PER] = lse2[j * PER:(j + 1) * PER]
        sown[j, PER:2 * PER] = delta[j * PER:(j + 1) * PER]

    pl.semaphore_wait(barrier, ROW - 1 + has_low.astype(jnp.int32) + has_high.astype(jnp.int32))

    def remote(src, dst, send, recv, target):
        return pltpu.make_async_remote_copy(
            src_ref=src, dst_ref=dst, send_sem=send, recv_sem=recv,
            device_id={"tok": target}, device_id_type=MESH,
        )

    def x_stat(d):
        to = (me + d) % ROW
        return remote(sown.at[to], sbuf.at[me + 2], ss.at[d], sr.at[d], mate(d))

    def x_q(d, h):
        to = (me + d) % ROW
        return remote(qown.at[to * PER + h], qbuf.at[me + 2, h], qs.at[d, h], qr.at[d, h], mate(d))

    def x_k(d, h):
        to = (me + d) % ROW
        return remote(kown.at[to * PER + h], kbuf.at[me, h], ks.at[d, h], kr.at[d, h], mate(d))

    def x_q_in(d, h):
        fr = (me + ROW - d) % ROW
        return remote(qown.at[0], qbuf.at[fr + 2, h], qs.at[d, h], qr.at[d, h], mate(d))

    def x_k_in(d, h):
        fr = (me + ROW - d) % ROW
        return remote(kown.at[0], kbuf.at[fr, h], ks.at[d, h], kr.at[d, h], mate(d))

    def x_stat_in(d):
        fr = (me + ROW - d) % ROW
        return remote(sown.at[0], sbuf.at[fr + 2], ss.at[d], sr.at[d], mate(d))

    order = (2, 1, 3)
    for d in order:
        x_stat(d).start()

    @pl.loop(0, PER)
    def _(h):
        for d in order:
            x_q(d, h).start()
        for d in order:
            x_k(d, h).start()

    @pl.loop(0, PER)
    def _(h):
        qbuf[me + 2, h] = qown[me * PER + h]
        kbuf[me, h] = kown[me * PER + h]

    sbuf[me + 2] = sown[me]

    @pl.when(jnp.logical_not(has_low))
    def _():
        dqr[0] = jnp.zeros(dqr.shape[1:], BF16)

    @pl.when(jnp.logical_not(has_high))
    def _():
        dqr[1] = jnp.zeros(dqr.shape[1:], BF16)

    def z_q(side, h):
        first, there = (2, 6) if side == 0 else (4, 0)
        target = tok - ROW if side == 0 else tok + ROW
        return remote(qbuf.at[pl.ds(first, 2), h], qbuf.at[pl.ds(there, 2), h],
                      zs.at[side, h], zr.at[1 - side, h], target)

    def z_q_in(side, h):
        here = 0 if side == 0 else 6
        target = tok - ROW if side == 0 else tok + ROW
        return remote(qbuf.at[pl.ds(here, 2), h], qbuf.at[pl.ds(here, 2), h],
                      zs.at[side, h], zr.at[side, h], target)

    def z_stat(side):
        first, there = (2, 6) if side == 0 else (4, 0)
        target = tok - ROW if side == 0 else tok + ROW
        return remote(sbuf.at[pl.ds(first, 2)], sbuf.at[pl.ds(there, 2)],
                      zss.at[side], zsr.at[1 - side], target)

    def z_stat_in(side):
        here = 0 if side == 0 else 6
        target = tok - ROW if side == 0 else tok + ROW
        return remote(sbuf.at[pl.ds(here, 2)], sbuf.at[pl.ds(here, 2)],
                      zss.at[side], zsr.at[side], target)

    def z_dq(side, h):
        target = tok - ROW if side == 0 else tok + ROW
        return remote(dqs.at[side, h], dqr.at[1 - side, h],
                      ds.at[side, h], dr.at[1 - side, h], target)

    def z_dq_in(side, h):
        target = tok - ROW if side == 0 else tok + ROW
        return remote(dqs.at[side, h], dqr.at[side, h],
                      ds.at[side, h], dr.at[side, h], target)

    def o_out(b, h):
        d = (b - me + ROW) % ROW
        return remote(obuf.at[b, h], orecv.at[me * PER + h],
                      os.at[d, h], orr.at[d, h], row * ROW + b)

    def o_in(d, h):
        fr = (me + ROW - d) % ROW
        return remote(obuf.at[0, h], orecv.at[fr * PER + h],
                      os.at[d, h], orr.at[d, h], mate(d))

    sides = ((0, has_low), (1, has_high))

    def sided(fn):
        for side, there in sides:
            @pl.when(there)
            def _():
                fn(side)

    for d in order:
        x_stat_in(d).wait_recv()
    sided(lambda side: z_stat(side).start())

    def task(c, slot, h, keys, values, keys_t):
        block = row * ROW + (slot - 2)
        flag = keep_ref[block, c + 4 - slot]
        gone = (1 - flag).astype(F32) * 1e30
        q_t, g_t = qbuf[slot, h, 0], qbuf[slot, h, 1]
        lse = sbuf[slot, pl.ds(h, 1), :] + gone
        delta = sbuf[slot, pl.ds(h + PER, 1), :]
        probs = jnp.exp2(dot_nn(keys, q_t) * (scale * LOG2E) - lse)
        grad = (probs * (dot_nn(values, g_t) - delta)).astype(BF16)
        return (
            dot_nn(keys_t, grad),
            dot_nt(q_t, grad),
            dot_nt(g_t, probs.astype(BF16)),
        )

    def run(h, work):
        seen = set()
        for c, slots, fresh in work:
            keys_t = kbuf[c, h, 0]
            keys = keys_t.T
            values = kbuf[c, h, 1].T
            dk = dv = None
            for slot in slots:
                tq, tk, tv = task(c, slot, h, keys, values, keys_t)
                dk = tk if dk is None else dk + tk
                dv = tv if dv is None else dv + tv
                if slot in seen:
                    dq[h, slot] += tq
                else:
                    dq[h, slot] = tq
                    seen.add(slot)
            if fresh:
                dkv[h, c, 0] = dk
                dkv[h, c, 1] = dv
            else:
                dkv[h, c, 0] += dk
                dkv[h, c, 1] += dv

    inner = ((0, (2, 3, 4), True), (1, (2, 3, 4, 5), True), (2, (2, 3, 4, 5), True), (3, (3, 4, 5), True))
    outer = (
        ((0, (0, 1), False), (1, (1,), False)),
        ((2, (6,), False), (3, (6, 7), False)),
    )

    def halo(side, h):
        z_q_in(side, h).wait_recv()
        run(h, outer[side])
        first = 0 if side == 0 else 6
        dqs[side, h] = (dq[h, pl.ds(first, 2)] * scale).astype(BF16)
        z_dq(side, h).start()

    def finish(h):
        sided(lambda side: z_dq_in(side, h).wait_recv())
        for b in range(ROW):
            total = dq[h, b + 2] * scale + dqr[b // 2, h, b % 2].astype(F32)
            obuf[b, h, 0] = total.astype(BF16)
            obuf[b, h, 1] = (dkv[h, b, 0] * scale).astype(BF16)
            obuf[b, h, 2] = dkv[h, b, 1].astype(BF16)

            @pl.when(b != me)
            def _():
                o_out(b, h).start()

            @pl.when(b == me)
            def _():
                orecv[me * PER + h] = obuf[b, h]

    @pl.loop(0, PER)
    def _(h):
        for d in order:
            x_q_in(d, h).wait_recv()
        sided(lambda side: z_q(side, h).start())
        for d in order:
            x_k_in(d, h).wait_recv()
        run(h, inner)

        @pl.when(h > 0)
        def _():
            finish(h - 1)

        @pl.when(h == 0)
        def _():
            sided(lambda side: z_stat_in(side).wait_recv())

        sided(lambda side: halo(side, h))

    finish(PER - 1)

    for d in order:
        x_stat(d).wait_send()
    sided(lambda side: z_stat(side).wait_send())

    @pl.loop(0, PER)
    def _(h):
        for d in order:
            x_q(d, h).wait_send()
            x_k(d, h).wait_send()
            o_in(d, h).wait_send()
            o_in(d, h).wait_recv()
        sided(lambda side: z_q(side, h).wait_send())
        sided(lambda side: z_dq(side, h).wait_send())

    for i, out in enumerate((dq_out, dk_out, dv_out)):
        out[...] = orecv[:, i].reshape(width, out.shape[0]).T


def per_device(count, query_rows, key_rows, value_rows, out_rows, grad_out, normalizer, keep_tasks):
    block, width = query_rows.shape
    dim = width // HEADS
    vmem = pl.BlockSpec(memory_space=pltpu.VMEM)
    dma = pltpu.SemaphoreType.DMA
    return pl.pallas_call(
        functools.partial(kernel, count),
        out_shape=[jax.ShapeDtypeStruct((block, width), BF16)] * 3,
        in_specs=[vmem] * 6 + [pl.BlockSpec(memory_space=pltpu.SMEM)],
        out_specs=[vmem] * 3,
        scratch_shapes=[
            pltpu.VMEM((HEADS, 2, dim, block), BF16),
            pltpu.VMEM((HEADS, 2, dim, block), BF16),
            pltpu.VMEM((ROW, 2 * PER, block), F32),
            pltpu.VMEM((ROW, PER, 2, dim, block), BF16),
            pltpu.VMEM((ROW + 4, PER, 2, dim, block), BF16),
            pltpu.VMEM((ROW + 4, 2 * PER, block), F32),
            pltpu.VMEM((PER, ROW + 4, dim, block), F32),
            pltpu.VMEM((PER, ROW, 2, dim, block), F32),
            pltpu.VMEM((2, PER, 2, dim, block), BF16),
            pltpu.VMEM((2, PER, 2, dim, block), BF16),
            pltpu.VMEM((ROW, PER, 3, dim, block), BF16),
            pltpu.VMEM((HEADS, 3, dim, block), BF16),
            dma((ROW, PER)), dma((ROW, PER)),
            dma((ROW, PER)), dma((ROW, PER)),
            dma((ROW,)), dma((ROW,)),
            dma((2, PER)), dma((2, PER)),
            dma((2,)), dma((2,)),
            dma((2, PER)), dma((2, PER)),
            dma((ROW, PER)), dma((ROW, PER)),
        ],
        compiler_params=pltpu.CompilerParams(
            collective_id=0, has_side_effects=True, vmem_limit_bytes=60 * 1024 * 1024
        ),
    )(query_rows, key_rows, value_rows, out_rows, grad_out, normalizer, keep_tasks)


def solution(mesh):
    rows = P(("groups", "tok"), None)
    return jax.shard_map(
        functools.partial(per_device, mesh.shape["tok"]),
        mesh=mesh,
        in_specs=(rows,) * 5 + (P(None, ("groups", "tok")), P("groups", None)),
        out_specs=(rows,) * 3,
        check_vma=False,
    )
```

time: 204 us -> 52.2 us (0.26)
  the two profiles are of different devices: /device:TPU:9 before, /device:TPU:1 now
where the time goes in v1:
time: 52.2 us; the launch traced here: 52 us
  Pallas kernels  46.2 us (89%)
  local copies, waits for them, and re-layouts  5.06 us (10%)
  between operations  0.65 us (1%)
    pallas_call x1, Pallas kernels, per_device(): pl.pallas_call(functools.partial(kernel, count), out_shape=[jax.ShapeDtyp...  46.2 us
    unnamed x8, local copies, waits for them, and re-layouts  5.06 us

profile of v1, /device:TPU:1, one launch (start us, length us, event | category | flops | bytes accessed | tf_op | source)
XLA Modules:
  0.0 52.0 jit_solution(11157728377558687060)
XLA Ops:
  0.6 1.4 %copy.10.keep_ref = s32[16,5]{1,0:T(8,128)} copy(s32[16,5]{0,1:T(8,128)} %param.13) | data formatting | bytes 640 | tf_op args[6]
  2.0 46.2 %shard_map.94 = (bf16[256,768]{1,0:T(8,128)(2,1)}, bf16[256,768]{1,0:T(8,128)(2,1)}, bf16[256,768]{1,0:T(8,128)(2,1)}) custom-call(bf16[256,768]{1,0:T(8,128)(2,1)} %q_ref.1, bf16[256,768]{1,0:T(8,128)(2,1)} %k_ref.1, bf16[256,768]{1,0:T(8,128)(2,1)} %v_ref.1, bf16[256,768]{1,0:T(8,128)(2,1)} %o_ref.1, bf16[256,768]{1,0:T(8,128)(2,1)} %g_ref.1, ...), custom_call_target="tpu_custom_call" | custom-call | tf_op jit(solution)/shard_map/pallas_call | solution.py:299
  48.2 0.0 copy-start.1
  48.2 1.8 %copy.14 = bf16[256,768]{1,0:T(8,128)(2,1)} copy(bf16[256,768]{1,0:T(8,128)(2,1)} %get-tuple-element.6) | data formatting | bytes 786432
  50.1 0.0 copy-done.1
  50.1 0.0 copy-start
  50.1 0.7 %copy.15 = bf16[256,768]{1,0:T(8,128)(2,1)} copy(bf16[256,768]{1,0:T(8,128)(2,1)S(1)} %copy-done.1) | data formatting | bytes 786432
  50.8 0.4 copy-done
  51.2 0.7 %copy.16 = bf16[256,768]{1,0:T(8,128)(2,1)} copy(bf16[256,768]{1,0:T(8,128)(2,1)S(1)} %copy-done) | data formatting | bytes 786432
Async XLA Ops:
  48.2 1.8 %copy-start.1 = (bf16[256,768]{1,0:T(8,128)(2,1)S(1)}, bf16[256,768]{1,0:T(8,128)(2,1)}, u32[]{:S(2)}) copy-start(bf16[256,768]{1,0:T(8,128)(2,1)} %get-tuple-element.7) | copy-start | bytes 1179652
  50.1 1.1 %copy-start = (bf16[256,768]{1,0:T(8,128)(2,1)S(1)}, bf16[256,768]{1,0:T(8,128)(2,1)}, u32[]{:S(2)}) copy-start(bf16[256,768]{1,0:T(8,128)(2,1)} %get-tuple-element.8) | copy-start | bytes 1179652

commit v2 on v1

--- a/solution.py
+++ b/solution.py
@@ -26,8 +26,8 @@
 
 def kernel(
     count, q_ref, k_ref, v_ref, o_ref, g_ref, lse_ref, keep_ref,
-    dq_out, dk_out, dv_out,
-    kown, qown, sown, kbuf, qbuf, sbuf, dq, dkv, dqs, dqr, obuf, orecv,
+    orecv,
+    kown, qown, sown, kbuf, qbuf, sbuf, dq, dkv, dqs, dqr, obuf,
     ks, kr, qs, qr, ss, sr, zs, zr, zss, zsr, ds, dr, os, orr,
 ):
     tok = lax.axis_index("tok")
@@ -187,7 +187,7 @@
 
     def task(c, slot, h, keys, values, keys_t):
         block = row * ROW + (slot - 2)
-        flag = keep_ref[block, c + 4 - slot]
+        flag = keep_ref[pl.ds(block, 1), c + 4 - slot:c + 5 - slot]
         gone = (1 - flag).astype(F32) * 1e30
         q_t, g_t = qbuf[slot, h, 0], qbuf[slot, h, 1]
         lse = sbuf[slot, pl.ds(h, 1), :] + gone
@@ -287,8 +287,10 @@
         sided(lambda side: z_q(side, h).wait_send())
         sided(lambda side: z_dq(side, h).wait_send())
 
-    for i, out in enumerate((dq_out, dk_out, dv_out)):
-        out[...] = orecv[:, i].reshape(width, out.shape[0]).T
+
+def unpack(packed_ref, *outs):
+    for i, out in enumerate(outs):
+        out[...] = packed_ref[:, i].reshape(out.shape[1], out.shape[0]).T
 
 
 def per_device(count, query_rows, key_rows, value_rows, out_rows, grad_out, normalizer, keep_tasks):
@@ -296,11 +298,11 @@
     dim = width // HEADS
     vmem = pl.BlockSpec(memory_space=pltpu.VMEM)
     dma = pltpu.SemaphoreType.DMA
-    return pl.pallas_call(
+    packed = pl.pallas_call(
         functools.partial(kernel, count),
-        out_shape=[jax.ShapeDtypeStruct((block, width), BF16)] * 3,
-        in_specs=[vmem] * 6 + [pl.BlockSpec(memory_space=pltpu.SMEM)],
-        out_specs=[vmem] * 3,
+        out_shape=jax.ShapeDtypeStruct((HEADS, 3, dim, block), BF16),
+        in_specs=[vmem] * 7,
+        out_specs=vmem,
         scratch_shapes=[
             pltpu.VMEM((HEADS, 2, dim, block), BF16),
             pltpu.VMEM((HEADS, 2, dim, block), BF16),
@@ -313,7 +315,6 @@
             pltpu.VMEM((2, PER, 2, dim, block), BF16),
             pltpu.VMEM((2, PER, 2, dim, block), BF16),
             pltpu.VMEM((ROW, PER, 3, dim, block), BF16),
-            pltpu.VMEM((HEADS, 3, dim, block), BF16),
             dma((ROW, PER)), dma((ROW, PER)),
             dma((ROW, PER)), dma((ROW, PER)),
             dma((ROW,)), dma((ROW,)),
@@ -326,6 +327,12 @@
             collective_id=0, has_side_effects=True, vmem_limit_bytes=60 * 1024 * 1024
         ),
     )(query_rows, key_rows, value_rows, out_rows, grad_out, normalizer, keep_tasks)
+    return pl.pallas_call(
+        unpack,
+        out_shape=[jax.ShapeDtypeStruct((block, width), BF16)] * 3,
+        in_specs=[vmem],
+        out_specs=[vmem] * 3,
+    )(packed)
 
 
 def solution(mesh):

time: 52.2 us -> 50.7 us (0.971)
  local copies, waits for them, and re-layouts: 5.06 us -> 1.36 us
  Pallas kernels: 46.2 us -> 48.4 us
    unnamed x8 -> x1, local copies, waits for them, and re-layouts: 5.06 us -> 1.36 us
    pallas_call x1 -> x2, Pallas kernels: 46.2 us -> 48.4 us  [the longest x1 46 us: per_device(): pl.pallas_call(functools.partial(kernel, count), out_shape=jax.ShapeDtype...]
where the time goes in v2:
time: 50.7 us; the launch traced here: 50.4 us
  Pallas kernels  48.4 us (95%)
  local copies, waits for them, and re-layouts  1.36 us (3%)
  between operations  0.64 us (1%)
    pallas_call x1, Pallas kernels, per_device(): pl.pallas_call(functools.partial(kernel, count), out_shape=jax.ShapeDtype...  46 us
    pallas_call x1, Pallas kernels, per_device(): pl.pallas_call(unpack, out_shape=[jax.ShapeDtypeStruct((block, width), BF...  2.43 us
    unnamed x1, local copies, waits for them, and re-layouts  1.36 us

profile of v2, /device:TPU:1, one launch (start us, length us, event | category | flops | bytes accessed | tf_op | source)
XLA Modules:
  0.0 50.4 jit_solution(8327034378616594966)
XLA Ops:
  0.6 1.4 %copy.10.keep_ref = s32[16,5]{1,0:T(8,128)} copy(s32[16,5]{0,1:T(8,128)} %param.13) | data formatting | bytes 640 | tf_op args[6]
  2.0 46.0 %shard_map.94.packed_ref = bf16[16,3,48,256]{3,2,1,0:T(8,128)(2,1)} custom-call(bf16[256,768]{1,0:T(8,128)(2,1)} %q_ref.1, bf16[256,768]{1,0:T(8,128)(2,1)} %k_ref.1, bf16[256,768]{1,0:T(8,128)(2,1)} %v_ref.1, bf16[256,768]{1,0:T(8,128)(2,1)} %o_ref.1, bf16[256,768]{1,0:T(8,128)(2,1)} %g_ref.1, f32[16,256]{1,0:T(8,128)} %lse_ref.1, s32[16,5]{1,0:T(8,128)} %copy.10.keep_ref), custom_call_target="tpu_custom_call" | custom-call | tf_op jit(solution)/shard_map/pallas_call | solution.py:301
  48.0 2.4 %shard_map.95 = (bf16[256,768]{1,0:T(8,128)(2,1)}, bf16[256,768]{1,0:T(8,128)(2,1)}, bf16[256,768]{1,0:T(8,128)(2,1)}) custom-call(bf16[16,3,48,256]{3,2,1,0:T(8,128)(2,1)} %shard_map.94.packed_ref), custom_call_target="tpu_custom_call" | custom-call | tf_op jit(solution)/shard_map/pallas_call | solution.py:330

commit v3 on v2

--- a/solution.py
+++ b/solution.py
@@ -194,34 +194,30 @@
         delta = sbuf[slot, pl.ds(h + PER, 1), :]
         probs = jnp.exp2(dot_nn(keys, q_t) * (scale * LOG2E) - lse)
         grad = (probs * (dot_nn(values, g_t) - delta)).astype(BF16)
-        return (
-            dot_nn(keys_t, grad),
-            dot_nt(q_t, grad),
-            dot_nt(g_t, probs.astype(BF16)),
-        )
+        return q_t, g_t, grad, probs.astype(BF16)
 
     def run(h, work):
-        seen = set()
+        pieces = {}
         for c, slots, fresh in work:
             keys_t = kbuf[c, h, 0]
             keys = keys_t.T
             values = kbuf[c, h, 1].T
-            dk = dv = None
-            for slot in slots:
-                tq, tk, tv = task(c, slot, h, keys, values, keys_t)
-                dk = tk if dk is None else dk + tk
-                dv = tv if dv is None else dv + tv
-                if slot in seen:
-                    dq[h, slot] += tq
-                else:
-                    dq[h, slot] = tq
-                    seen.add(slot)
+            parts = [task(c, slot, h, keys, values, keys_t) for slot in slots]
+            q_all, g_all, grads, lows = [jnp.concatenate([p[i] for p in parts], axis=1) for i in range(4)]
+            dk, dv = dot_nt(q_all, grads), dot_nt(g_all, lows)
+            for slot, p in zip(slots, parts):
+                pieces.setdefault(slot, []).append((keys_t, p[2]))
             if fresh:
                 dkv[h, c, 0] = dk
                 dkv[h, c, 1] = dv
             else:
                 dkv[h, c, 0] += dk
                 dkv[h, c, 1] += dv
+        for slot, terms in pieces.items():
+            dq[h, slot] = dot_nn(
+                jnp.concatenate([t[0] for t in terms], axis=1),
+                jnp.concatenate([t[1] for t in terms], axis=0),
+            )
 
     inner = ((0, (2, 3, 4), True), (1, (2, 3, 4, 5), True), (2, (2, 3, 4, 5), True), (3, (3, 4, 5), True))
     outer = (

time: 50.7 us -> 45.6 us (0.90)
  Pallas kernels: 48.4 us -> 43.4 us
    pallas_call x1, Pallas kernels: 46 us -> 41 us  [per_device(): pl.pallas_call(functools.partial(kernel, count), out_shape=jax.ShapeDtype...]
where the time goes in v3:
time: 45.6 us; the launch traced here: 45.4 us
  Pallas kernels  43.4 us (95%)
  local copies, waits for them, and re-layouts  1.36 us (3%)
  between operations  0.64 us (1%)
    pallas_call x1, Pallas kernels, per_device(): pl.pallas_call(functools.partial(kernel, count), out_shape=jax.ShapeDtype...  41 us
    pallas_call x1, Pallas kernels, per_device(): pl.pallas_call(unpack, out_shape=[jax.ShapeDtypeStruct((block, width), BF...  2.43 us
    unnamed x1, local copies, waits for them, and re-layouts  1.36 us

profile of v3, /device:TPU:1, one launch (start us, length us, event | category | flops | bytes accessed | tf_op | source)
XLA Modules:
  0.0 45.4 jit_solution(2271466467405348105)
XLA Ops:
  0.6 1.4 %copy.10.keep_ref = s32[16,5]{1,0:T(8,128)} copy(s32[16,5]{0,1:T(8,128)} %param.13) | data formatting | bytes 640 | tf_op args[6]
  2.0 41.0 %shard_map.94.packed_ref = bf16[16,3,48,256]{3,2,1,0:T(8,128)(2,1)} custom-call(bf16[256,768]{1,0:T(8,128)(2,1)} %q_ref.1, bf16[256,768]{1,0:T(8,128)(2,1)} %k_ref.1, bf16[256,768]{1,0:T(8,128)(2,1)} %v_ref.1, bf16[256,768]{1,0:T(8,128)(2,1)} %o_ref.1, bf16[256,768]{1,0:T(8,128)(2,1)} %g_ref.1, f32[16,256]{1,0:T(8,128)} %lse_ref.1, s32[16,5]{1,0:T(8,128)} %copy.10.keep_ref), custom_call_target="tpu_custom_call" | custom-call | tf_op jit(solution)/shard_map/pallas_call | solution.py:297
  43.0 2.4 %shard_map.95 = (bf16[256,768]{1,0:T(8,128)(2,1)}, bf16[256,768]{1,0:T(8,128)(2,1)}, bf16[256,768]{1,0:T(8,128)(2,1)}) custom-call(bf16[16,3,48,256]{3,2,1,0:T(8,128)(2,1)} %shard_map.94.packed_ref), custom_call_target="tpu_custom_call" | custom-call | tf_op jit(solution)/shard_map/pallas_call | solution.py:326
